TPU v7x, 256 devices: a whole 4x4x8 slice. The times are simulated.
256 devices in a mesh: half: 2 (over core), dev: 128 (over y, x, z).
Axes of the slice: x: 4, y: 4, z: 8, core: 2. Of those that a mesh axis runs over, the one named last changes fastest.
Arguments:
- field_mix: float32 [32, 32], P('half'), may hold values from -1 to 1
- alm: bfloat16 [1024, 2, 32, 2048], P('dev', None, 'half'), may hold values from -6 to 6
- legendre: bfloat16 [1024, 2048, 128], P('dev'), may hold values from -0.125 to 0.125
- order_ids: int32 [1024], replicated, may hold values from 0 to 1023, each once
- fetch_list: int32 [128, 128, 2], replicated, may hold values from -1 to 31, as said below
- scan_tiles: int32 [512, 32], P('dev'), may hold values from 0 to 255, as said below
- block_tile: int32 [512, 32], P('dev'), may hold values from 0 to 31
- block_pix: int32 [512, 16384], P('dev'), may hold values from -1 to 127, as said below
- noise_kernel: float32 [512, 512], P('dev'), may hold values from -0.24 to 0.24
- scan_weight: float32 [512], P('dev'), may hold values from 0.1 to 1
Outputs:
- binned: float32 [128, 32, 4096], P('dev', 'half')
Inputs may be any that keep to these rules, and one draw needn't show every extreme that they name: `fetch_list`: entry [d, e, k] is the index, among the 32 tiles of device d, of the tile that device e fetches from d in slot k, or -1 for an empty slot; the live slots of one pair come first and name distinct tiles; every device fills all 2 slots from at least one source. `scan_tiles`: entry [n, i] is a slot source 2 + k whose fetch_list[source, n div 4, k] is not -1. `block_pix`: -1 marks a flagged sample.
All inputs are finite; a program needn't handle non-finite values.
Results may differ from a plain program's by a relative error of at most 0.007.
Values may be sent and summed in bfloat16 or wider, within the bound.
No kernel may reach another device: no remote copies, remote signals or barrier semaphores. Data moves between devices by JAX's collectives and lax.ppermute only.
A program may use at most 128 MiB of HBM per device.

v0:
```python
import math
import jax
import jax.numpy as jnp
from jax import lax
from jax.sharding import PartitionSpec as P

NPHI = 4096
TILE = 128
BLK = 512


def toeplitz_rows(band_values, block_len):
    scan_count = band_values.shape[0]
    wrapped = jnp.pad(band_values, ((0, 0), (0, 1)))
    repeated = jnp.tile(wrapped, (1, block_len))
    folded = repeated[:, : block_len * (2 * block_len - 1)].reshape(
        scan_count, block_len, 2 * block_len - 1
    )
    return folded[:, :, block_len - 1 :]


def local(
    field_mix,
    alm,
    legendre,
    order_ids,
    fetch_list,
    scan_tiles,
    block_tile,
    block_pix,
    noise_kernel,
    scan_weight,
):
    highest = lax.Precision.HIGHEST
    device_count = lax.axis_size("dev")
    position = lax.axis_index("dev")
    both_halves = lax.all_gather(alm, "half", axis=2, tiled=True)
    mixed_alm = jnp.einsum(
        "fg,scgl->scfl", field_mix, both_halves.astype(jnp.float32), precision=highest
    ).astype(jnp.bfloat16)
    cycle_coeff = jnp.einsum(
        "scfl,slr->rscf", mixed_alm, legendre, preferred_element_type=jnp.float32
    ).astype(jnp.bfloat16)
    by_cycle = lax.all_to_all(cycle_coeff, "dev", split_axis=0, concat_axis=1, tiled=True)
    cycle_count = by_cycle.shape[0]
    order_count = by_cycle.shape[1]
    field_count = by_cycle.shape[3]
    pixel_block = 512
    block_count = NPHI // pixel_block
    weights = jnp.where(order_ids == 0, 1.0, 2.0).astype(jnp.float32) / math.sqrt(2.0 * order_count)

    def cycle_block(start):
        pixel_iota = start + jnp.arange(pixel_block, dtype=jnp.int32)
        phase_steps = order_ids[:, None] * (2 * pixel_iota[None, :] + 1) % (2 * NPHI)
        angles = phase_steps.astype(jnp.float32) * (math.pi / NPHI)
        fourier = jnp.stack(
            [weights[:, None] * jnp.cos(angles), -weights[:, None] * jnp.sin(angles)], axis=1
        ).astype(jnp.bfloat16)
        return jnp.einsum(
            "rscf,scj->rfj", by_cycle, fourier, preferred_element_type=jnp.float32
        ).astype(jnp.bfloat16)

    starts = jnp.arange(block_count, dtype=jnp.int32) * pixel_block
    cycle_blocks = lax.map(cycle_block, starts)
    per_block = pixel_block // TILE
    map_tiles = cycle_blocks.reshape(block_count, cycle_count, field_count, per_block, TILE)
    map_tiles = map_tiles.transpose(1, 0, 3, 2, 4).reshape(
        cycle_count * block_count * per_block, field_count, TILE
    )
    tile_count = map_tiles.shape[0]
    slot_capacity = fetch_list.shape[2]
    owner_row = lax.dynamic_index_in_dim(fetch_list, position, 0, keepdims=False)
    every_tile = lax.all_gather(map_tiles, "dev", axis=0, tiled=True)
    my_column = lax.dynamic_index_in_dim(fetch_list, position, 1, keepdims=False)
    global_ids = jnp.arange(device_count, dtype=jnp.int32)[:, None] * tile_count + jnp.maximum(
        my_column, 0
    )
    fetched = every_tile[global_ids] * (my_column >= 0).astype(jnp.bfloat16)[:, :, None, None]
    slot_total = device_count * slot_capacity
    flat_fetched = fetched.reshape(slot_total, field_count, TILE)
    scan_count = block_tile.shape[0]
    block_total = block_tile.shape[1]
    slot_index = jnp.take_along_axis(scan_tiles, block_tile, axis=1)
    block_tiles = flat_fetched[slot_index]
    pixels = block_pix.reshape(scan_count, block_total, BLK)
    one_hot = (
        pixels[:, :, None, :] == jnp.arange(TILE, dtype=jnp.int32)[None, None, :, None]
    ).astype(jnp.bfloat16)
    samples = jnp.einsum(
        "sbfp,sbpt->sbft", block_tiles, one_hot, preferred_element_type=jnp.float32
    ).astype(jnp.bfloat16)
    taps = noise_kernel.astype(jnp.bfloat16)
    near_band = jnp.concatenate([taps[:, ::-1], taps[:, 1:]], axis=1)
    far_band = jnp.concatenate(
        [jnp.zeros((scan_count, BLK), jnp.bfloat16), taps[:, 1:][:, ::-1]], axis=1
    )
    near_table = toeplitz_rows(near_band, BLK)
    far_table = toeplitz_rows(far_band, BLK)
    earlier = jnp.pad(samples[:, :-1], ((0, 0), (1, 0), (0, 0), (0, 0)))
    later = jnp.pad(samples[:, 1:], ((0, 0), (0, 1), (0, 0), (0, 0)))
    filtered = jnp.einsum("sbfu,stu->sbft", samples, near_table, preferred_element_type=jnp.float32)
    filtered = filtered + jnp.einsum(
        "sbfu,stu->sbft", earlier, far_table, preferred_element_type=jnp.float32
    )
    filtered = filtered + jnp.einsum(
        "sbfu,sut->sbft", later, far_table, preferred_element_type=jnp.float32
    )
    weighted = (scan_weight[:, None, None, None] * filtered).astype(jnp.bfloat16)
    partial_value = jnp.einsum(
        "sbft,sbpt->sbfp", weighted, one_hot, preferred_element_type=jnp.float32
    )
    flat_slots = slot_index.reshape(-1)
    slot_select = (jnp.arange(slot_total, dtype=jnp.int32)[:, None] == flat_slots[None, :]).astype(
        jnp.float32
    )
    per_slot = jnp.dot(
        slot_select,
        partial_value.reshape(scan_count * block_total, field_count * TILE),
        precision=highest,
    )
    per_slot = per_slot.reshape(device_count, slot_capacity, field_count, TILE)
    returned = lax.all_to_all(per_slot, "dev", split_axis=0, concat_axis=0, tiled=True)
    owner_select = (
        jnp.arange(tile_count, dtype=jnp.int32)[:, None] == owner_row.reshape(-1)[None, :]
    ).astype(jnp.float32)
    own_tiles = jnp.dot(
        owner_select, returned.reshape(slot_total, field_count * TILE), precision=highest
    )
    binned = own_tiles.reshape(cycle_count, NPHI // TILE, field_count, TILE).transpose(0, 2, 1, 3)
    return binned.reshape(cycle_count, field_count, NPHI)


def solution(mesh):
    return jax.shard_map(
        local,
        mesh=mesh,
        in_specs=(
            P("half", None),
            P("dev", None, "half", None),
            P("dev", None, None),
            P(),
            P(),
            P("dev", None),
            P("dev", None),
            P("dev", None),
            P("dev", None),
            P("dev"),
        ),
        out_specs=P("dev", "half", None),
        check_vma=False,
    )
```

profile of v0, /device:TPU:32, one launch (start us, length us, event | category | flops | bytes accessed | tf_op | source)
XLA Modules:
  0.0 397.4 jit_solution(6174108100497894636)
XLA Ops:
  7.3 20.4 %all-gather.3.cloned.1.call-done = bf16[8,2,32,2048]{3,2,1,0:T(8,128)(2,1)} async-done(((bf16[8,2,16,2048]{3,2,1,0:T(8,128)(2,1)}), bf16[8,2,32,2048]{3,2,1,0:T(8,128)(2,1)}) %all-gather.3.cloned.1.call-update) | async-done | bytes 2097168 | tf_op jit(solution)/shard_map/all_gather | solution.py:37
  34.9 13.7 %all-to-all-start = ((bf16[128,2,128]{2,1,0:T(2,128)(2,1)}), bf16[128,2,128]{2,1,0:T(2,128)(2,1)S(1)}, u32[]{:S(2)}, u32[]{:S(2)}) async-start(bf16[128,2,128]{2,1,0:T(2,128)(2,1)} %reshape.451), calls=%async_computation | async-start | bytes 131072 | tf_op jit(solution)/shard_map/all_to_all | solution.py:44
  49.2 10.5 %all-to-all-done = bf16[128,2,128]{2,1,0:T(2,128)(2,1)S(1)} async-done(((bf16[128,2,128]{2,1,0:T(2,128)(2,1)}), bf16[128,2,128]{2,1,0:T(2,128)(2,1)S(1)}, u32[]{:S(2)}, u32[]{:S(2)}) %all-to-all-start) | async-done | bytes 65568 | tf_op jit(solution)/shard_map/all_to_all | solution.py:44
  60.4 88.3 %while.12 = (s32[]{:T(128)}, bf16[8,1,16,512]{3,2,1,0:T(8,128)(2,1)S(1)}, f32[1024]{0:T(1024)S(1)}, s32[1024]{0:T(1024)S(1)}, s32[8]{0:T(128)S(1)}, /*index=5*/f...) while((s32[]{:T(128)}, bf16[8,1,16,512]{3,2,1,0:T(8,128)(2,1)S(1)}, f32[1024]{0:T(1024)S(1)}, ...), condition=%wide.region_1.2_spmd, body=%wide.region_0.1_spmd.sunk | while | flops 44049920 | bytes 4292721 | solution.py:64
  61.6 9.4 %multiply_convert_fusion.4 = (bf16[1024,1,512]{2,0,1:T(8,128)(2,1)S(1)}, bf16[1024,1,512]{2,0,1:T(8,128)(2,1)S(1)}) fusion(s32[512]{0:T(512)S(1)} %multiply_add_fusion.3, s32[1024]{0:T(1024)S(1)} %get-tuple-element.204, f32[1024]{0:T(1024)S(1)} %get-tuple-element.203, f32[1024]{0:T(1024)S(1)} %bitcast.147), kind=kLoop, calls=%fused_computation.16.clone.1 | loop fusion | flops 9437184 | bytes 2111488 | tf_op jit(solution)/shard_map/convert
  72.7 9.4 %multiply_convert_fusion.4 = (bf16[1024,1,512]{2,0,1:T(8,128)(2,1)S(1)}, bf16[1024,1,512]{2,0,1:T(8,128)(2,1)S(1)}) fusion(s32[512]{0:T(512)S(1)} %multiply_add_fusion.3, s32[1024]{0:T(1024)S(1)} %get-tuple-element.204, f32[1024]{0:T(1024)S(1)} %get-tuple-element.203, f32[1024]{0:T(1024)S(1)} %bitcast.147), kind=kLoop, calls=%fused_computation.16.clone.1 | loop fusion | flops 9437184 | bytes 2111488 | tf_op jit(solution)/shard_map/convert
  83.7 9.4 %multiply_convert_fusion.4 = (bf16[1024,1,512]{2,0,1:T(8,128)(2,1)S(1)}, bf16[1024,1,512]{2,0,1:T(8,128)(2,1)S(1)}) fusion(s32[512]{0:T(512)S(1)} %multiply_add_fusion.3, s32[1024]{0:T(1024)S(1)} %get-tuple-element.204, f32[1024]{0:T(1024)S(1)} %get-tuple-element.203, f32[1024]{0:T(1024)S(1)} %bitcast.147), kind=kLoop, calls=%fused_computation.16.clone.1 | loop fusion | flops 9437184 | bytes 2111488 | tf_op jit(solution)/shard_map/convert
  94.8 9.4 %multiply_convert_fusion.4 = (bf16[1024,1,512]{2,0,1:T(8,128)(2,1)S(1)}, bf16[1024,1,512]{2,0,1:T(8,128)(2,1)S(1)}) fusion(s32[512]{0:T(512)S(1)} %multiply_add_fusion.3, s32[1024]{0:T(1024)S(1)} %get-tuple-element.204, f32[1024]{0:T(1024)S(1)} %get-tuple-element.203, f32[1024]{0:T(1024)S(1)} %bitcast.147), kind=kLoop, calls=%fused_computation.16.clone.1 | loop fusion | flops 9437184 | bytes 2111488 | tf_op jit(solution)/shard_map/convert
  105.8 9.4 %multiply_convert_fusion.4 = (bf16[1024,1,512]{2,0,1:T(8,128)(2,1)S(1)}, bf16[1024,1,512]{2,0,1:T(8,128)(2,1)S(1)}) fusion(s32[512]{0:T(512)S(1)} %multiply_add_fusion.3, s32[1024]{0:T(1024)S(1)} %get-tuple-element.204, f32[1024]{0:T(1024)S(1)} %get-tuple-element.203, f32[1024]{0:T(1024)S(1)} %bitcast.147), kind=kLoop, calls=%fused_computation.16.clone.1 | loop fusion | flops 9437184 | bytes 2111488 | tf_op jit(solution)/shard_map/convert
  116.8 9.4 %multiply_convert_fusion.4 = (bf16[1024,1,512]{2,0,1:T(8,128)(2,1)S(1)}, bf16[1024,1,512]{2,0,1:T(8,128)(2,1)S(1)}) fusion(s32[512]{0:T(512)S(1)} %multiply_add_fusion.3, s32[1024]{0:T(1024)S(1)} %get-tuple-element.204, f32[1024]{0:T(1024)S(1)} %get-tuple-element.203, f32[1024]{0:T(1024)S(1)} %bitcast.147), kind=kLoop, calls=%fused_computation.16.clone.1 | loop fusion | flops 9437184 | bytes 2111488 | tf_op jit(solution)/shard_map/convert
  127.9 9.4 %multiply_convert_fusion.4 = (bf16[1024,1,512]{2,0,1:T(8,128)(2,1)S(1)}, bf16[1024,1,512]{2,0,1:T(8,128)(2,1)S(1)}) fusion(s32[512]{0:T(512)S(1)} %multiply_add_fusion.3, s32[1024]{0:T(1024)S(1)} %get-tuple-element.204, f32[1024]{0:T(1024)S(1)} %get-tuple-element.203, f32[1024]{0:T(1024)S(1)} %bitcast.147), kind=kLoop, calls=%fused_computation.16.clone.1 | loop fusion | flops 9437184 | bytes 2111488 | tf_op jit(solution)/shard_map/convert
  138.9 9.4 %multiply_convert_fusion.4 = (bf16[1024,1,512]{2,0,1:T(8,128)(2,1)S(1)}, bf16[1024,1,512]{2,0,1:T(8,128)(2,1)S(1)}) fusion(s32[512]{0:T(512)S(1)} %multiply_add_fusion.3, s32[1024]{0:T(1024)S(1)} %get-tuple-element.204, f32[1024]{0:T(1024)S(1)} %get-tuple-element.203, f32[1024]{0:T(1024)S(1)} %bitcast.147), kind=kLoop, calls=%fused_computation.16.clone.1 | loop fusion | flops 9437184 | bytes 2111488 | tf_op jit(solution)/shard_map/convert
  153.3 3.2 copy.59
  159.6 5.8 %reshape.447 = bf16[2095104]{0:T(1024)(128)(2,1)} reshape(bf16[4,523776]{1,0:T(4,128)(2,1)} %slice.36) | data formatting | bytes 8380416
  165.4 10.1 %reshape.402 = bf16[4,512,1023]{2,1,0:T(8,128)(2,1)} reshape(bf16[2095104]{0:T(1024)(128)(2,1)} %reshape.447) | data formatting | bytes 8380416 | tf_op jit(solution)/shard_map/reshape | solution.py:16
  176.6 3.2 copy.60
  183.0 5.7 %reshape.449 = bf16[2095104]{0:T(1024)(128)(2,1)} reshape(bf16[4,523776]{1,0:T(4,128)(2,1)} %slice.39) | data formatting | bytes 8380416
  188.7 10.1 %reshape.403 = bf16[4,512,1023]{2,1,0:T(8,128)(2,1)} reshape(bf16[2095104]{0:T(1024)(128)(2,1)} %reshape.449) | data formatting | bytes 8380416 | tf_op jit(solution)/shard_map/reshape | solution.py:16
  199.0 93.0 %all-gather.5.cloned.1.call-done = bf16[4096,16,128]{2,1,0:T(8,128)(2,1)} async-done(((bf16[32,16,128]{2,1,0:T(8,128)(2,1)}), bf16[4096,16,128]{2,1,0:T(8,128)(2,1)}) %all-gather.5.cloned.1.call-update) | async-done | bytes 16777232 | tf_op jit(solution)/shard_map/all_gather | solution.py:73
  292.0 6.6 %gather_fusion = bf16[256,16,128]{2,1,0:T(8,128)(2,1)S(1)} fusion(bf16[4096,16,128]{2,1,0:T(8,128)(2,1)} %all-gather.5.cloned.1.call-done, s32[1024]{0:T(1024)S(1)} %pad_clamp_fusion.1), kind=kCustom, calls=%fused_computation | custom fusion | bytes 2098176 | tf_op jit(solution)/shard_map/gather | solution.py:78
  299.6 5.4 %fusion.32 = bf16[4,32,16,512]{3,2,1,0:T(8,128)(2,1)S(1)} fusion(bf16[4,32,16,128]{3,2,1,0:T(8,128)(2,1)S(1)} %bitcast.140, s32[4,32,512]{2,1,0:T(8,128)S(1)} %bitcast.144), kind=kOutput, calls=%fused_computation.43 | convolution fusion | flops 277872640 | bytes 2883584 | tf_op jit(solution)/shard_map/sbfp,sbpt->sbft/dot_general | solution.py:89
  310.3 5.0 %fusion.21 = f32[4,32,16,128]{3,2,1,0:T(8,128)S(1)} fusion(bf16[4,32,16,512]{3,2,1,0:T(8,128)(2,1)S(1)} %multiply_convert_fusion.2, s32[4,32,512]{2,1,0:T(8,128)S(1)} %bitcast.145), kind=kOutput, calls=%fused_computation.25 | convolution fusion | flops 276824064 | bytes 3407872 | tf_op jit(solution)/shard_map/sbft,sbpt->sbfp/dot_general | solution.py:109
  319.6 11.5 %all-to-all-start.1 = ((f32[128,2,16,128]{3,2,1,0:T(8,128)}), f32[128,2,16,128]{3,2,1,0:T(8,128)S(1)}, u32[]{:S(2)}, u32[]{:S(2)}) async-start(f32[128,2,16,128]{3,2,1,0:T(8,128)} %copy.48), calls=%async_computation.1 | async-start | bytes 4194304 | tf_op jit(solution)/shard_map/all_to_all | solution.py:122
  331.4 52.8 %all-to-all-done.1 = f32[128,2,16,128]{3,2,1,0:T(8,128)S(1)} async-done(((f32[128,2,16,128]{3,2,1,0:T(8,128)}), f32[128,2,16,128]{3,2,1,0:T(8,128)S(1)}, u32[]{:S(2)}, u32[]{:S(2)}) %all-to-all-start.1) | async-done | bytes 2097184 | tf_op jit(solution)/shard_map/all_to_all | solution.py:122
  (104 shorter events, 50.9 us)
Async XLA Ops:
  6.5 143.4 %copy-start = (s32[128,128,2]{1,2,0:T(2,128)S(1)}, s32[128,128,2]{1,2,0:T(2,128)}, u32[]{:S(2)}) copy-start(s32[128,128,2]{1,2,0:T(2,128)} %param.16) | copy-start | bytes 393220
  6.5 21.1 %all-gather.3.cloned.1.call-start = ((), (), s32[]{:S(2)}) async-start(), calls=%async_computation.2 | async-start | bytes 3145728 | tf_op jit(solution)/shard_map/all_gather | solution.py:37
  30.4 18.7 %copy-start.5 = (s32[1024]{0:T(1024)S(1)}, s32[1024]{0:T(1024)}, u32[]{:S(2)}) copy-start(s32[1024]{0:T(1024)} %param.15) | copy-start | bytes 12292
  34.9 24.8 %all-to-all-start = ((bf16[128,2,128]{2,1,0:T(2,128)(2,1)}), bf16[128,2,128]{2,1,0:T(2,128)(2,1)S(1)}, u32[]{:S(2)}, u32[]{:S(2)}) async-start(bf16[128,2,128]{2,1,0:T(2,128)(2,1)} %reshape.451), calls=%async_computation | async-start | bytes 131072 | tf_op jit(solution)/shard_map/all_to_all | solution.py:44
  48.6 243.4 %all-gather.5.cloned.1.call-start = ((), (), s32[]{:S(2)}) async-start(), calls=%async_computation.3 | async-start | bytes 16908288 | tf_op jit(solution)/shard_map/all_gather | solution.py:73
  60.4 89.1 %copy-start.6 = (f32[4,512]{1,0:T(4,128)S(1)}, f32[4,512]{1,0:T(4,128)}, u32[]{:S(2)}) copy-start(f32[4,512]{1,0:T(4,128)} %param.20) | copy-start | bytes 24580
  60.4 90.5 %copy-start.7 = (s32[4,32]{1,0:T(4,128)S(1)}, s32[4,32]{1,0:T(4,128)}, u32[]{:S(2)}) copy-start(s32[4,32]{1,0:T(4,128)} %param.18) | copy-start | bytes 1540
  148.7 2.2 copy-start.1
  148.7 3.9 copy-start.4
  299.6 5.4 %copy-start.3 = (bf16[4,512,1023]{2,1,0:T(8,128)(2,1)S(1)}, bf16[4,512,1023]{2,1,0:T(8,128)(2,1)}, u32[]{:S(2)}) copy-start(bf16[4,512,1023]{2,1,0:T(8,128)(2,1)} %reshape.402) | copy-start | bytes 12570628
  305.0 2.2 copy-start.2
  307.2 1.4 copy-start.8
  319.6 64.6 %all-to-all-start.1 = ((f32[128,2,16,128]{3,2,1,0:T(8,128)}), f32[128,2,16,128]{3,2,1,0:T(8,128)S(1)}, u32[]{:S(2)}, u32[]{:S(2)}) async-start(f32[128,2,16,128]{3,2,1,0:T(8,128)} %copy.48), calls=%async_computation.1 | async-start | bytes 4194304 | tf_op jit(solution)/shard_map/all_to_all | solution.py:122
Sparse Core Ops, SparseCore 0:
  9.1 18.5 all-gather.2
  149.6 142.3 all-gather.4
where the time goes:
time: 402 us; the launch traced here: 397 us
  waiting for transfers between devices  177 us (44%)
  other arithmetic  80.8 us (20%)
  local copies, waits for them, and re-layouts  73.3 us (18%)
  matrix products  25.9 us (6%)
  starting transfers between devices  25.8 us (6%)
  between operations  14 us (3%)
    all_gather x1, waiting for transfers between devices, local(): every_tile = lax.all_gather(map_tiles, 'dev', axis=0, tiled=True)  93 us
    another operation x8, other arithmetic  75.2 us
    all_to_all x1, waiting for transfers between devices, local(): lax.all_to_all(per_slot, 'dev', split_axis=0, concat_axis=0, tiled=True)  52.8 us
    unnamed x32, local copies, waits for them, and re-layouts  24.5 us
    all_gather x1, waiting for transfers between devices, local(): both_halves = lax.all_gather(alm, 'half', axis=2, tiled=True)  20.4 us
    reshape x2, local copies, waits for them, and re-layouts, toeplitz_rows(): repeated[:, :block_len * (2 * block_len - 1)]  20.2 us
    all_to_all x1, starting transfers between devices, local(): lax.all_to_all(cycle_coeff, 'dev', split_axis=0, concat_axis=1, tiled=True)  13.7 us
    all_to_all x1, starting transfers between devices, local(): lax.all_to_all(per_slot, 'dev', split_axis=0, concat_axis=0, tiled=True)  11.5 us
  transfers between devices with their start and end apart: 4, of which 4 were waited for; matrix products, arithmetic and copies ran while one was open for 12% of the time, Pallas kernels for 0%

commit v1 on v0

--- a/solution.py
+++ b/solution.py
@@ -7,6 +7,16 @@
 NPHI = 4096
 TILE = 128
 BLK = 512
+
+
+def groups_keep_up(local_x, dim_no):
+    item_now = jax.lax.all_to_all(
+        jnp.stack(jax.lax.psum(1, axis_name="half") * [local_x]),
+        axis_name="half",
+        split_axis=0,
+        concat_axis=0,
+    )
+    return jnp.concatenate(item_now, axis=dim_no)
 
 
 def toeplitz_rows(band_values, block_len):
@@ -34,7 +44,7 @@
     highest = lax.Precision.HIGHEST
     device_count = lax.axis_size("dev")
     position = lax.axis_index("dev")
-    both_halves = lax.all_gather(alm, "half", axis=2, tiled=True)
+    both_halves = groups_keep_up(alm, 2)
     mixed_alm = jnp.einsum(
         "fg,scgl->scfl", field_mix, both_halves.astype(jnp.float32), precision=highest
     ).astype(jnp.bfloat16)

time: 402 us -> 387 us (0.963)
  waiting for transfers between devices: 177 us -> 156 us
  blocking collectives: 0 us -> 5.42 us
    all_gather x1 -> x0, waiting for transfers between devices: 20.4 us -> none  [local(): both_halves = lax.all_gather(alm, 'half', axis=2, tiled=True)]
    all_to_all x0 -> x1, blocking collectives: none -> 5.42 us  [groups_keep_up(): jax.lax.all_to_all(jnp.stack(jax.lax.psum(1, axis_name='half') * [local_x...]
    another operation x8 -> x9, other arithmetic: 75.2 us -> 77 us
    unnamed x32 -> x36, local copies, waits for them, and re-layouts: 24.5 us -> 25.2 us
  transfers between devices with their start and end apart: 4 -> 3, of which waited for: 4 -> 3; matrix products, arithmetic and copies ran while one was open for 12% -> 13% of each run, Pallas kernels for 0% -> 0%
where the time goes in v1:
time: 387 us; the launch traced here: 382 us
  waiting for transfers between devices  156 us (40%)
  other arithmetic  82.6 us (21%)
  local copies, waits for them, and re-layouts  74.3 us (19%)
  starting transfers between devices  27.1 us (7%)
  matrix products  22.1 us (6%)
  between operations  14.1 us (4%)
  blocking collectives  5.42 us (1%)
    all_gather x1, waiting for transfers between devices, local(): every_tile = lax.all_gather(map_tiles, 'dev', axis=0, tiled=True)  93 us
    another operation x8, other arithmetic  75.2 us
    all_to_all x1, waiting for transfers between devices, local(): lax.all_to_all(per_slot, 'dev', split_axis=0, concat_axis=0, tiled=True)  52.8 us
    unnamed x36, local copies, waits for them, and re-layouts  25.2 us
    reshape x2, local copies, waits for them, and re-layouts, toeplitz_rows(): repeated[:, :block_len * (2 * block_len - 1)]  20.2 us
    all_to_all x1, starting transfers between devices, local(): lax.all_to_all(cycle_coeff, 'dev', split_axis=0, concat_axis=1, tiled=True)  15 us
    all_to_all x1, starting transfers between devices, local(): lax.all_to_all(per_slot, 'dev', split_axis=0, concat_axis=0, tiled=True)  11.5 us
    all_to_all x1, waiting for transfers between devices, local(): lax.all_to_all(cycle_coeff, 'dev', split_axis=0, concat_axis=1, tiled=True)  10.5 us
  transfers between devices with their start and end apart: 3, of which 3 were waited for; matrix products, arithmetic and copies ran while one was open for 13% of the time, Pallas kernels for 0%

profile of v1, /device:TPU:32, one launch (start us, length us, event | category | flops | bytes accessed | tf_op | source)
XLA Modules:
  0.0 382.0 jit_solution(14745084841799736909)
XLA Ops:
  8.3 5.4 %all_to_all.22 = bf16[2,8,2,16,2048]{4,3,2,1,0:T(8,128)(2,1)S(1)} all-to-all(bf16[2,8,2,16,2048]{4,3,2,1,0:T(8,128)(2,1)S(1)} %pad_maximum_fusion), channel_id=1, replica_groups=mesh['half'=2,'dev'=128] {'half'}, dimensions={0} | all-to-all | bytes 4194304 | tf_op jit(solution)/shard_map/all_to_all | solution.py:13
  18.2 15.0 %all-to-all-start.1 = ((bf16[128,2,128]{2,1,0:T(2,128)(2,1)}), bf16[128,2,128]{2,1,0:T(2,128)(2,1)S(1)}, u32[]{:S(2)}, u32[]{:S(2)}) async-start(bf16[128,2,128]{2,1,0:T(2,128)(2,1)} %reshape.459), calls=%async_computation.1 | async-start | bytes 131072 | tf_op jit(solution)/shard_map/all_to_all | solution.py:54
  33.8 10.5 %all-to-all-done.1 = bf16[128,2,128]{2,1,0:T(2,128)(2,1)S(1)} async-done(((bf16[128,2,128]{2,1,0:T(2,128)(2,1)}), bf16[128,2,128]{2,1,0:T(2,128)(2,1)S(1)}, u32[]{:S(2)}, u32[]{:S(2)}) %all-to-all-start.1) | async-done | bytes 65568 | tf_op jit(solution)/shard_map/all_to_all | solution.py:54
  45.0 88.3 %while.12 = (s32[]{:T(128)}, bf16[8,1,16,512]{3,2,1,0:T(8,128)(2,1)S(1)}, f32[1024]{0:T(1024)S(1)}, s32[1024]{0:T(1024)S(1)}, s32[8]{0:T(128)S(1)}, /*index=5*/f...) while((s32[]{:T(128)}, bf16[8,1,16,512]{3,2,1,0:T(8,128)(2,1)S(1)}, f32[1024]{0:T(1024)S(1)}, ...), condition=%wide.region_1.2_spmd, body=%wide.region_0.1_spmd.sunk | while | flops 44049920 | bytes 4292721 | solution.py:74
  46.2 9.4 %multiply_convert_fusion.4 = (bf16[1024,1,512]{2,0,1:T(8,128)(2,1)S(1)}, bf16[1024,1,512]{2,0,1:T(8,128)(2,1)S(1)}) fusion(s32[512]{0:T(512)S(1)} %multiply_add_fusion.3, s32[1024]{0:T(1024)S(1)} %get-tuple-element.204, f32[1024]{0:T(1024)S(1)} %get-tuple-element.203, f32[1024]{0:T(1024)S(1)} %bitcast.153), kind=kLoop, calls=%fused_computation.16.clone.1 | loop fusion | flops 9437184 | bytes 2111488 | tf_op jit(solution)/shard_map/convert
  57.3 9.4 %multiply_convert_fusion.4 = (bf16[1024,1,512]{2,0,1:T(8,128)(2,1)S(1)}, bf16[1024,1,512]{2,0,1:T(8,128)(2,1)S(1)}) fusion(s32[512]{0:T(512)S(1)} %multiply_add_fusion.3, s32[1024]{0:T(1024)S(1)} %get-tuple-element.204, f32[1024]{0:T(1024)S(1)} %get-tuple-element.203, f32[1024]{0:T(1024)S(1)} %bitcast.153), kind=kLoop, calls=%fused_computation.16.clone.1 | loop fusion | flops 9437184 | bytes 2111488 | tf_op jit(solution)/shard_map/convert
  68.3 9.4 %multiply_convert_fusion.4 = (bf16[1024,1,512]{2,0,1:T(8,128)(2,1)S(1)}, bf16[1024,1,512]{2,0,1:T(8,128)(2,1)S(1)}) fusion(s32[512]{0:T(512)S(1)} %multiply_add_fusion.3, s32[1024]{0:T(1024)S(1)} %get-tuple-element.204, f32[1024]{0:T(1024)S(1)} %get-tuple-element.203, f32[1024]{0:T(1024)S(1)} %bitcast.153), kind=kLoop, calls=%fused_computation.16.clone.1 | loop fusion | flops 9437184 | bytes 2111488 | tf_op jit(solution)/shard_map/convert
  79.4 9.4 %multiply_convert_fusion.4 = (bf16[1024,1,512]{2,0,1:T(8,128)(2,1)S(1)}, bf16[1024,1,512]{2,0,1:T(8,128)(2,1)S(1)}) fusion(s32[512]{0:T(512)S(1)} %multiply_add_fusion.3, s32[1024]{0:T(1024)S(1)} %get-tuple-element.204, f32[1024]{0:T(1024)S(1)} %get-tuple-element.203, f32[1024]{0:T(1024)S(1)} %bitcast.153), kind=kLoop, calls=%fused_computation.16.clone.1 | loop fusion | flops 9437184 | bytes 2111488 | tf_op jit(solution)/shard_map/convert
  90.4 9.4 %multiply_convert_fusion.4 = (bf16[1024,1,512]{2,0,1:T(8,128)(2,1)S(1)}, bf16[1024,1,512]{2,0,1:T(8,128)(2,1)S(1)}) fusion(s32[512]{0:T(512)S(1)} %multiply_add_fusion.3, s32[1024]{0:T(1024)S(1)} %get-tuple-element.204, f32[1024]{0:T(1024)S(1)} %get-tuple-element.203, f32[1024]{0:T(1024)S(1)} %bitcast.153), kind=kLoop, calls=%fused_computation.16.clone.1 | loop fusion | flops 9437184 | bytes 2111488 | tf_op jit(solution)/shard_map/convert
  101.5 9.4 %multiply_convert_fusion.4 = (bf16[1024,1,512]{2,0,1:T(8,128)(2,1)S(1)}, bf16[1024,1,512]{2,0,1:T(8,128)(2,1)S(1)}) fusion(s32[512]{0:T(512)S(1)} %multiply_add_fusion.3, s32[1024]{0:T(1024)S(1)} %get-tuple-element.204, f32[1024]{0:T(1024)S(1)} %get-tuple-element.203, f32[1024]{0:T(1024)S(1)} %bitcast.153), kind=kLoop, calls=%fused_computation.16.clone.1 | loop fusion | flops 9437184 | bytes 2111488 | tf_op jit(solution)/shard_map/convert
  112.5 9.4 %multiply_convert_fusion.4 = (bf16[1024,1,512]{2,0,1:T(8,128)(2,1)S(1)}, bf16[1024,1,512]{2,0,1:T(8,128)(2,1)S(1)}) fusion(s32[512]{0:T(512)S(1)} %multiply_add_fusion.3, s32[1024]{0:T(1024)S(1)} %get-tuple-element.204, f32[1024]{0:T(1024)S(1)} %get-tuple-element.203, f32[1024]{0:T(1024)S(1)} %bitcast.153), kind=kLoop, calls=%fused_computation.16.clone.1 | loop fusion | flops 9437184 | bytes 2111488 | tf_op jit(solution)/shard_map/convert
  123.5 9.4 %multiply_convert_fusion.4 = (bf16[1024,1,512]{2,0,1:T(8,128)(2,1)S(1)}, bf16[1024,1,512]{2,0,1:T(8,128)(2,1)S(1)}) fusion(s32[512]{0:T(512)S(1)} %multiply_add_fusion.3, s32[1024]{0:T(1024)S(1)} %get-tuple-element.204, f32[1024]{0:T(1024)S(1)} %get-tuple-element.203, f32[1024]{0:T(1024)S(1)} %bitcast.153), kind=kLoop, calls=%fused_computation.16.clone.1 | loop fusion | flops 9437184 | bytes 2111488 | tf_op jit(solution)/shard_map/convert
  137.9 3.2 copy.61
  144.2 5.7 %reshape.455 = bf16[2095104]{0:T(1024)(128)(2,1)} reshape(bf16[4,523776]{1,0:T(4,128)(2,1)} %slice.36) | data formatting | bytes 8380416
  150.0 10.1 %reshape.410 = bf16[4,512,1023]{2,1,0:T(8,128)(2,1)} reshape(bf16[2095104]{0:T(1024)(128)(2,1)} %reshape.455) | data formatting | bytes 8380416 | tf_op jit(solution)/shard_map/reshape | solution.py:26
  161.2 3.2 copy.62
  167.6 5.7 %reshape.457 = bf16[2095104]{0:T(1024)(128)(2,1)} reshape(bf16[4,523776]{1,0:T(4,128)(2,1)} %slice.39) | data formatting | bytes 8380416
  173.3 10.1 %reshape.411 = bf16[4,512,1023]{2,1,0:T(8,128)(2,1)} reshape(bf16[2095104]{0:T(1024)(128)(2,1)} %reshape.457) | data formatting | bytes 8380416 | tf_op jit(solution)/shard_map/reshape | solution.py:26
  183.5 93.0 %all-gather.2.cloned.1.call-done = bf16[4096,16,128]{2,1,0:T(8,128)(2,1)} async-done(((bf16[32,16,128]{2,1,0:T(8,128)(2,1)}), bf16[4096,16,128]{2,1,0:T(8,128)(2,1)}) %all-gather.2.cloned.1.call-update) | async-done | bytes 16777232 | tf_op jit(solution)/shard_map/all_gather | solution.py:83
  276.6 6.6 %gather_fusion = bf16[256,16,128]{2,1,0:T(8,128)(2,1)S(1)} fusion(bf16[4096,16,128]{2,1,0:T(8,128)(2,1)} %all-gather.2.cloned.1.call-done, s32[1024]{0:T(1024)S(1)} %pad_clamp_fusion.1), kind=kCustom, calls=%fused_computation | custom fusion | bytes 2098176 | tf_op jit(solution)/shard_map/gather | solution.py:88
  284.2 5.4 %fusion.32 = bf16[4,32,16,512]{3,2,1,0:T(8,128)(2,1)S(1)} fusion(bf16[4,32,16,128]{3,2,1,0:T(8,128)(2,1)S(1)} %bitcast.146, s32[4,32,512]{2,1,0:T(8,128)S(1)} %bitcast.150), kind=kOutput, calls=%fused_computation.44 | convolution fusion | flops 277872640 | bytes 2883584 | tf_op jit(solution)/shard_map/sbfp,sbpt->sbft/dot_general | solution.py:99
  294.9 5.0 %fusion.21 = f32[4,32,16,128]{3,2,1,0:T(8,128)S(1)} fusion(bf16[4,32,16,512]{3,2,1,0:T(8,128)(2,1)S(1)} %multiply_convert_fusion.2, s32[4,32,512]{2,1,0:T(8,128)S(1)} %bitcast.151), kind=kOutput, calls=%fused_computation.25 | convolution fusion | flops 276824064 | bytes 3407872 | tf_op jit(solution)/shard_map/sbft,sbpt->sbfp/dot_general | solution.py:119
  304.2 11.5 %all-to-all-start.2 = ((f32[128,2,16,128]{3,2,1,0:T(8,128)}), f32[128,2,16,128]{3,2,1,0:T(8,128)S(1)}, u32[]{:S(2)}, u32[]{:S(2)}) async-start(f32[128,2,16,128]{3,2,1,0:T(8,128)} %copy.50), calls=%async_computation.2 | async-start | bytes 4194304 | tf_op jit(solution)/shard_map/all_to_all | solution.py:132
  316.0 52.8 %all-to-all-done.2 = f32[128,2,16,128]{3,2,1,0:T(8,128)S(1)} async-done(((f32[128,2,16,128]{3,2,1,0:T(8,128)}), f32[128,2,16,128]{3,2,1,0:T(8,128)S(1)}, u32[]{:S(2)}, u32[]{:S(2)}) %all-to-all-start.2) | async-done | bytes 2097184 | tf_op jit(solution)/shard_map/all_to_all | solution.py:132
  (108 shorter events, 49.2 us)
Async XLA Ops:
  6.5 128.0 %copy-start = (s32[128,128,2]{1,2,0:T(2,128)S(1)}, s32[128,128,2]{1,2,0:T(2,128)}, u32[]{:S(2)}) copy-start(s32[128,128,2]{1,2,0:T(2,128)} %param.16) | copy-start | bytes 393220
  8.3 5.7 %copy-start.7 = (f32[16,32]{1,0:T(8,128)S(1)}, f32[16,32]{1,0:T(8,128)}, u32[]{:S(2)}) copy-start(f32[16,32]{1,0:T(8,128)} %param.12) | copy-start | bytes 6148
  13.7 2.2 copy-start.4
  15.9 17.8 %copy-start.6 = (s32[1024]{0:T(1024)S(1)}, s32[1024]{0:T(1024)}, u32[]{:S(2)}) copy-start(s32[1024]{0:T(1024)} %param.15) | copy-start | bytes 12292
  18.2 26.1 %all-to-all-start.1 = ((bf16[128,2,128]{2,1,0:T(2,128)(2,1)}), bf16[128,2,128]{2,1,0:T(2,128)(2,1)S(1)}, u32[]{:S(2)}, u32[]{:S(2)}) async-start(bf16[128,2,128]{2,1,0:T(2,128)(2,1)} %reshape.459), calls=%async_computation.1 | async-start | bytes 131072 | tf_op jit(solution)/shard_map/all_to_all | solution.py:54
  33.2 243.4 %all-gather.2.cloned.1.call-start = ((), (), s32[]{:S(2)}) async-start(), calls=%async_computation.3 | async-start | bytes 16908288 | tf_op jit(solution)/shard_map/all_gather | solution.py:83
  45.0 89.1 %copy-start.8 = (f32[4,512]{1,0:T(4,128)S(1)}, f32[4,512]{1,0:T(4,128)}, u32[]{:S(2)}) copy-start(f32[4,512]{1,0:T(4,128)} %param.20) | copy-start | bytes 24580
  45.0 90.5 %copy-start.9 = (s32[4,32]{1,0:T(4,128)S(1)}, s32[4,32]{1,0:T(4,128)}, u32[]{:S(2)}) copy-start(s32[4,32]{1,0:T(4,128)} %param.18) | copy-start | bytes 1540
  133.3 2.2 copy-start.1
  133.3 3.9 %copy-start.5 = (s32[4,16384]{1,0:T(4,128)S(1)}, s32[4,16384]{1,0:T(4,128)}, u32[]{:S(2)}) copy-start(s32[4,16384]{1,0:T(4,128)} %param.19) | copy-start | bytes 786436
  284.2 5.4 %copy-start.3 = (bf16[4,512,1023]{2,1,0:T(8,128)(2,1)S(1)}, bf16[4,512,1023]{2,1,0:T(8,128)(2,1)}, u32[]{:S(2)}) copy-start(bf16[4,512,1023]{2,1,0:T(8,128)(2,1)} %reshape.410) | copy-start | bytes 12570628
  289.6 2.2 copy-start.2
  291.8 1.4 copy-start.10
  304.2 64.6 %all-to-all-start.2 = ((f32[128,2,16,128]{3,2,1,0:T(8,128)}), f32[128,2,16,128]{3,2,1,0:T(8,128)S(1)}, u32[]{:S(2)}, u32[]{:S(2)}) async-start(f32[128,2,16,128]{3,2,1,0:T(8,128)} %copy.50), calls=%async_computation.2 | async-start | bytes 4194304 | tf_op jit(solution)/shard_map/all_to_all | solution.py:132
Sparse Core Ops, SparseCore 0:
  134.2 142.3 all-gather.1
